TPU v7x, 32 devices: a whole 2x2x4 slice. The times are simulated.
32 devices in a mesh: row: 16 (over z, y, core), col: 2 (over x).
Axes of the slice: x: 2, y: 2, z: 4, core: 2. Of those that a mesh axis runs over, the one named last changes fastest.
Arguments:
- seq: float32 [768, 1024], P('row', 'col'), may hold values from -6 to 6
- query: float32 [768, 1024], P('row', 'col'), may hold values from -24 to 24, as said below
- key: float32 [768, 1024], P('col', 'row'), may hold values from -24 to 24, as said below
- value: float32 [768, 1024], P('col', 'row'), may hold values from -6 to 6
- pair: float32 [768, 768, 128], P('row', 'col'), may hold values from -6 to 6
- w_bias: float32 [128, 32], replicated, may hold values from -0.5 to 0.5
- w_out: float32 [1024, 1024], P(None, 'col'), may hold values from -0.75 to 0.75
- w_left: float32 [1024, 64], P('col'), may hold values from -0.1875 to 0.1875
- w_right: float32 [1024, 64], P('col'), may hold values from -0.1875 to 0.1875
- w_outer: float32 [128, 128], replicated, may hold values from -0.5 to 0.5
- outer_bias: float32 [128], replicated, may hold values from -3 to 3
- w_up: float32 [128, 512], replicated, may hold values from -0.5 to 0.5
- w_down: float32 [512, 128], replicated, may hold values from -0.25 to 0.25
Outputs:
- seq_new: float32 [768, 1024], P('row', 'col')
- pair_new: float32 [768, 768, 128], P('row', 'col')
Inputs may be any that keep to these rules, and one draw needn't show every extreme that they name: `query`: Head-major queries of order one; some residues may be much larger. `key`: Head-major keys of order one; some residues may be much larger.
All inputs are finite; a program needn't handle non-finite values.
Results may differ from a plain program's by a relative error of at most 0.0003.
Values sent between devices are 32-bit elements; how exact they have to be, the bound alone decides.
A program may use at most 128 MiB of HBM per device.

v0:
```python
import functools

import jax
import jax.numpy as jnp
from jax import lax
from jax.experimental import pallas as pl
from jax.experimental.pallas import tpu as pltpu
from jax.sharding import PartitionSpec as P

HIGH = lax.Precision.HIGHEST
F32 = jnp.float32
BF16 = jnp.bfloat16
VMEM_LIMIT = 60 * 1024 * 1024
MESH = pl.DeviceIdType.MESH


def halves(x):
    high = x.astype(BF16)
    low = (x - high.astype(F32)).astype(BF16)
    return high, low


def split(x):
    kept = lax.reduce_precision(x, 8, 7)
    return kept.astype(BF16), (x - kept).astype(BF16)


def channel_norm(x):
    centre = x - jnp.mean(x, axis=-1, keepdims=True)
    return centre * lax.rsqrt(jnp.mean(centre * centre, axis=-1, keepdims=True) + 1e-05)


def dot_nt(a, b, precision=None):
    return lax.dot_general(
        a, b, (((1,), (1,)), ((), ())), precision=precision, preferred_element_type=F32
    )


def gather_attention_kernel(
    n, n_col, head_dim, heads,
    kv_ref, q_ref, pair_ref, wt_hi_ref, wt_lo_ref,
    part_ref, stat_ref,
    kv_buf, q_buf, bias_buf, pair_buf,
    recv_sem, z_sem, y_sem, core_sem, q_send, q_recv, pair_sem,
):
    n_z = n // 4
    n_slot, rows, wide = q_ref.shape
    groups, group = pair_buf.shape[:2]
    per = wide // 2 // head_dim
    row, col = lax.axis_index("row"), lax.axis_index("col")
    core, y = lax.rem(row, 2), lax.rem(lax.div(row, 2), 2)
    core_peer, y_peer = row + 1 - 2 * core, row + 2 - 4 * y
    z_peers = [lax.rem(row + 4 * k, n) for k in range(1, n_z)]
    col_peers = [lax.rem(col + k, n_col) for k in range(1, n_col)]

    def pair_copy(g):
        return pltpu.make_async_copy(
            pair_ref.at[pl.ds(g * group, group)], pair_buf.at[g], pair_sem.at[g]
        )

    for g in range(groups):
        pair_copy(g).start()
    own_kv = pltpu.make_async_copy(kv_ref, kv_buf.at[row], recv_sem.at[row])
    own_kv.start()
    own_q = pltpu.make_async_copy(
        q_ref, q_buf.at[pl.ds(col * n_slot, n_slot)], q_recv.at[col]
    )
    own_q.start()

    barrier = pltpu.get_barrier_semaphore()
    for peer in z_peers + [y_peer, core_peer]:
        pl.semaphore_signal(barrier, inc=1, device_id={"row": peer}, device_id_type=MESH)
    for peer in col_peers:
        pl.semaphore_signal(barrier, inc=1, device_id={"col": peer}, device_id_type=MESH)
    pl.semaphore_wait(barrier, n_z + n_col)

    def put(src, slot, sem, peer):
        return pltpu.make_async_remote_copy(
            src_ref=src,
            dst_ref=kv_buf.at[slot],
            send_sem=sem,
            recv_sem=recv_sem.at[slot],
            device_id={"row": peer},
            device_id_type=MESH,
        )

    def put_q(slot_col, peer, sem):
        return pltpu.make_async_remote_copy(
            src_ref=q_ref,
            dst_ref=q_buf.at[pl.ds(slot_col * n_slot, n_slot)],
            send_sem=sem,
            recv_sem=q_recv.at[slot_col],
            device_id={"col": peer},
            device_id_type=MESH,
        )

    order = [0]
    for k in range(1, n_z // 2 + 1):
        order += [k] if 2 * k == n_z else [k, n_z - k]
    put(kv_ref, row, y_sem.at[0], y_peer).start()
    for t in range(1, n_z):
        put(kv_ref, row, z_sem.at[t], z_peers[order[t] - 1]).start()
    put(kv_ref, row, core_sem.at[0], core_peer).start()
    for k, peer in enumerate(col_peers):
        put_q(col, peer, q_send.at[k]).start()
    own_kv.wait()
    own_q.wait()

    def slot_z(t):
        return lax.rem(row - 4 * order[t] + n, n)

    def relay_z(t):
        slot = slot_z(t)
        put(kv_buf.at[slot], slot, y_sem.at[t], y_peer).wait_recv()
        put(kv_buf.at[slot], slot, y_sem.at[t], y_peer).start()
        put(kv_buf.at[slot], slot, core_sem.at[2 * t], core_peer).start()

    def relay_y(t):
        slot = slot_z(t) + 2 - 4 * y
        put(kv_buf.at[slot], slot, core_sem.at[2 * t + 1], core_peer).wait_recv()
        put(kv_buf.at[slot], slot, core_sem.at[2 * t + 1], core_peer).start()

    def bias_group(g, carry):
        pair_copy(g).wait()
        parts = [halves(channel_norm(pair_buf[g, i])) for i in range(group)]
        high = jnp.concatenate([p[0] for p in parts], axis=1)
        low = jnp.concatenate([p[1] for p in parts], axis=1)
        wt_hi = wt_hi_ref[...]
        flat = dot_nt(wt_hi, high) + (dot_nt(wt_hi, low) + dot_nt(wt_lo_ref[...], high))
        bias_buf[:, pl.ds(pl.multiple_of(g * group, group), group), :] = flat.reshape(
            heads, group, flat.shape[1]
        )
        return carry

    for t in range(1, n_z):
        lax.fori_loop(
            (t - 1) * groups // (n_z - 1), t * groups // (n_z - 1), bias_group, 0
        )
        relay_z(t)
        relay_y(t - 1)
    for k in range(1, n_col):
        source = lax.rem(col - k + n_col, n_col)
        put_q(source, col_peers[k - 1], q_send.at[k - 1]).wait_recv()

    scale = F32(head_dim) ** -0.5
    lane = lax.broadcasted_iota(jnp.int32, (rows, wide), 1) // head_dim
    stat_lane = lax.broadcasted_iota(jnp.int32, (rows, stat_ref.shape[2]), 1)
    dot = functools.partial(jnp.dot, preferred_element_type=F32)
    stat_ref[...] = jnp.zeros_like(stat_ref)

    def attend(base):
        part = jnp.zeros((rows, wide), F32)
        for par in range(2):
            slot = base + par
            k_at, v_at = (per, 0) if par == 0 else (0, per)
            q = q_buf[slot]
            kv = kv_buf[slot]
            qs = jnp.concatenate(
                [jnp.where(lane == k_at + m, q, 0.0) for m in range(per)], axis=0
            )
            bias = bias_buf[pl.ds(slot * per, per)].reshape(per * rows, -1)
            scores = dot_nt(qs, kv, HIGH) * scale + bias
            top = jnp.max(scores, axis=1, keepdims=True)
            expo = jnp.exp(scores - top)
            total = jnp.sum(expo, axis=1, keepdims=True)
            e_hi, e_lo = halves(expo)
            v_hi, v_lo = halves(kv)
            out = dot(e_hi, v_hi) + (dot(e_hi, v_lo) + dot(e_lo, v_hi))
            for m in range(per):
                mine = slice(m * rows, (m + 1) * rows)
                part = jnp.where(lane == v_at + m, out[mine], part)
                here = stat_lane == slot * per + m
                stat_ref[0] = jnp.where(here, top[mine], stat_ref[0])
                stat_ref[1] = jnp.where(here, total[mine], stat_ref[1])
        part_ref[lax.div(base, 2)] = part

    for t in range(n_z):
        if t == n_z - 1:
            relay_y(t)

        def chip(u, carry):
            base = slot_z(t) - core + u * (2 - 4 * y)
            slot = base + 1 - core
            put(kv_buf.at[slot], slot, core_sem.at[0], core_peer).wait_recv()
            attend(base)
            return carry

        lax.fori_loop(0, 2, chip, 0)

    for t in range(n_z):
        slot = slot_z(t)
        if t:
            put(kv_ref, slot, z_sem.at[t], y_peer).wait_send()
        put(kv_ref, slot, y_sem.at[t], y_peer).wait_send()
        for u in range(2):
            put(kv_ref, slot, core_sem.at[2 * t + u], core_peer).wait_send()
    for k, peer in enumerate(col_peers):
        put_q(col, peer, q_send.at[k]).wait_send()


def gather_attention(query, key, value, pair, w_bias):
    n, n_col = lax.axis_size("row"), lax.axis_size("col")
    rows, cols, channels = pair.shape
    heads = w_bias.shape[1]
    feats = key.shape[1]
    head_dim = feats * n // heads
    n_slot = query.shape[1] // feats
    group = 8
    eye = jnp.eye(group, dtype=F32)
    wt = (w_bias.T[:, None, None, :] * eye[None, :, :, None]).reshape(
        heads * group, group * channels
    )
    wt_hi, wt_lo = split(wt)
    odd = lax.rem(lax.axis_index("row"), 2) == 1
    kv = jnp.where(
        odd, jnp.concatenate([key, value], axis=1), jnp.concatenate([value, key], axis=1)
    )
    q = query.reshape(rows, n_slot // 2, 2, feats).transpose(1, 2, 0, 3)
    zero = jnp.zeros_like(q[:, 0])
    q = jnp.stack(
        [jnp.concatenate([zero, q[:, 0]], axis=2), jnp.concatenate([q[:, 1], zero], axis=2)],
        axis=1,
    ).reshape(n_slot, rows, 2 * feats)
    any_space = pl.BlockSpec(memory_space=pl.ANY)
    vmem = pl.BlockSpec(memory_space=pltpu.VMEM)
    dma = pltpu.SemaphoreType.DMA
    n_z = n // 4
    return pl.pallas_call(
        functools.partial(gather_attention_kernel, n, n_col, head_dim, heads),
        out_shape=(
            jax.ShapeDtypeStruct((n // 2, rows, 2 * feats), F32),
            jax.ShapeDtypeStruct((2, rows, 128), F32),
        ),
        in_specs=[any_space, any_space, any_space, vmem, vmem],
        out_specs=(vmem, vmem),
        scratch_shapes=[
            pltpu.VMEM((n, cols, 2 * feats), F32),
            pltpu.VMEM((n, rows, 2 * feats), F32),
            pltpu.VMEM((heads, rows, cols), F32),
            pltpu.VMEM((rows // group, group, cols, channels), F32),
            dma((n,)),
            dma((n_z,)),
            dma((n_z,)),
            dma((2 * n_z,)),
            dma((n_col,)),
            dma((n_col,)),
            dma((rows // group,)),
        ],
        compiler_params=pltpu.CompilerParams(
            vmem_limit_bytes=VMEM_LIMIT, collective_id=0, has_side_effects=True
        ),
        name="gather_attention",
    )(kv, q, pair, wt_hi, wt_lo)


def merge_kernel(
    n, n_col, head_dim, heads,
    part_ref, stat_ref, seq_ref, w_out_ref, w_both_ref,
    seq_out, left_out, right_out,
    part_buf, stat_buf, packet, packet_buf, both_buf, right_buf,
    part_send, part_recv, stat_send, stat_recv, pack_send, pack_recv,
    right_send, right_recv, relay_send,
):
    rows, here = seq_ref.shape
    width = w_out_ref.shape[0]
    proj = left_out.shape[1]
    blocks = right_buf.shape[0]
    row, col = lax.axis_index("row"), lax.axis_index("col")
    core = lax.rem(row, 2)
    core_peer = row + 1 - 2 * core
    col_peers = [lax.rem(col + k, n_col) for k in range(1, n_col)]
    row_peers = [lax.rem(row + 2 * k, n) for k in range(1, n // 2)]

    barrier = pltpu.get_barrier_semaphore()
    for peer in row_peers + [core_peer]:
        pl.semaphore_signal(barrier, inc=1, device_id={"row": peer}, device_id_type=MESH)
    for peer in col_peers:
        pl.semaphore_signal(barrier, inc=1, device_id={"col": peer}, device_id_type=MESH)
    pl.semaphore_wait(barrier, n // 2 + n_col - 1)

    def put(src, dst, send, recv, peer):
        return pltpu.make_async_remote_copy(
            src_ref=src, dst_ref=dst, send_sem=send, recv_sem=recv,
            device_id=peer, device_id_type=MESH,
        )

    def over_col(src, buf, send, recv):
        return [
            put(src, buf.at[k], send.at[k], recv.at[k], {"col": peer})
            for k, peer in enumerate(col_peers)
        ]

    stats = over_col(stat_ref, stat_buf, stat_send, stat_recv)
    parts = over_col(part_ref, part_buf, part_send, part_recv)
    for copy in stats + parts:
        copy.start()
    for copy in stats:
        copy.wait()
    tops = [stat_ref[0]] + [stat_buf[k, 0] for k in range(n_col - 1)]
    totals = [stat_ref[1]] + [stat_buf[k, 1] for k in range(n_col - 1)]
    highest = functools.reduce(jnp.maximum, tops)
    scales = [jnp.exp(top - highest) for top in tops]
    total = sum(scale * t for scale, t in zip(scales, totals))
    lane = lax.broadcasted_iota(jnp.int32, total.shape, 1)
    total = jnp.where(lane < heads, total, 1.0)
    spread_of = (
        lax.broadcasted_iota(jnp.int32, (total.shape[1], width), 0)
        == lax.broadcasted_iota(jnp.int32, (total.shape[1], width), 1) // head_dim
    ).astype(F32)
    weights = [
        jnp.dot(scale / total, spread_of, precision=HIGH, preferred_element_type=F32)
        for scale in scales
    ]
    for copy in parts:
        copy.wait()

    def dense(load):
        return jnp.concatenate([load(m) for m in range(part_ref.shape[0])], axis=1)

    attn = dense(lambda m: part_ref[m]) * weights[0]
    for k in range(n_col - 1):
        attn = attn + dense(lambda m: part_buf[k, m]) * weights[k + 1]
    seq_new = seq_ref[...] + jnp.dot(
        attn, w_out_ref[...], precision=HIGH, preferred_element_type=F32
    )
    seq_out[...] = seq_new

    local_mean = jnp.mean(seq_new, axis=1, keepdims=True)
    centred = seq_new - local_mean
    spread = jnp.sum(centred * centred, axis=1, keepdims=True)
    w_both = w_both_ref[...]
    packet[:rows] = jnp.dot(centred, w_both, precision=HIGH, preferred_element_type=F32)
    lane = lax.broadcasted_iota(jnp.int32, (rows, 2 * proj), 1)
    packet[rows : 2 * rows] = jnp.where(lane < proj, local_mean, spread)
    packet[2 * rows :] = jnp.broadcast_to(
        jnp.sum(w_both, axis=0, keepdims=True), (8, 2 * proj)
    )
    packets = over_col(packet, packet_buf, pack_send, pack_recv)
    for copy in packets:
        copy.start()
    for copy in packets:
        copy.wait()
    every = [packet[...]] + [packet_buf[k] for k in range(n_col - 1)]
    means = [p[rows : 2 * rows, :1] for p in every]
    mean = sum(means) / n_col
    offsets = [m - mean for m in means]
    variance = (
        sum(p[rows : 2 * rows, proj : proj + 1] for p in every)
        + here * sum(o * o for o in offsets)
    ) / width
    both = sum(p[:rows] + o * p[2 * rows : 2 * rows + 1] for p, o in zip(every, offsets))
    both = both * lax.rsqrt(variance + 1e-05)
    left_out[...] = both[:, :proj]
    both_buf[...] = both

    mine = lax.div(row, blocks) == col
    own = lax.rem(row, blocks)

    def row_copies():
        return [
            put(both_buf, right_buf.at[own], right_send.at[k], right_recv.at[own], {"row": peer})
            for k, peer in enumerate(row_peers)
        ]

    @pl.when(mine)
    def _():
        for copy in row_copies():
            copy.start()
        keep = pltpu.make_async_copy(both_buf, right_buf.at[own], right_recv.at[own])
        keep.start()
        keep.wait()

    def relay(j, block):
        slot = right_buf.at[block]
        return put(slot, slot, relay_send.at[j], right_recv.at[block], {"row": core_peer})

    for j in range(blocks // 2):
        block = 2 * j + core

        @pl.when(col * blocks + block != row)
        def _():
            relay(j, block).wait_recv()

        relay(j, block).start()
    for j in range(blocks // 2):
        relay(j, 2 * j + 1 - core).wait_recv()
    for b in range(blocks):
        right_out[b * rows : (b + 1) * rows] = right_buf[b][:, proj:]
    for j in range(blocks // 2):
        relay(j, 2 * j + core).wait_send()

    @pl.when(mine)
    def _():
        for copy in row_copies():
            copy.wait_send()


def merge(part, stat, seq, w_out, w_left, w_right, head_dim, heads, cols):
    n, n_col = lax.axis_size("row"), lax.axis_size("col")
    rows = seq.shape[0]
    proj = w_left.shape[1]
    blocks = cols // rows
    w_both = jnp.concatenate([w_left, w_right], axis=1)
    vmem = pl.BlockSpec(memory_space=pltpu.VMEM)
    dma = pltpu.SemaphoreType.DMA
    peers = n_col - 1
    return pl.pallas_call(
        functools.partial(merge_kernel, n, n_col, head_dim, heads),
        out_shape=(
            jax.ShapeDtypeStruct(seq.shape, F32),
            jax.ShapeDtypeStruct((rows, proj), F32),
            jax.ShapeDtypeStruct((cols, proj), F32),
        ),
        in_specs=[vmem] * 5,
        out_specs=(vmem,) * 3,
        scratch_shapes=[
            pltpu.VMEM((peers, *part.shape), F32),
            pltpu.VMEM((peers, *stat.shape), F32),
            pltpu.VMEM((2 * rows + 8, 2 * proj), F32),
            pltpu.VMEM((peers, 2 * rows + 8, 2 * proj), F32),
            pltpu.VMEM((rows, 2 * proj), F32),
            pltpu.VMEM((blocks, rows, 2 * proj), F32),
            dma((peers,)), dma((peers,)), dma((peers,)), dma((peers,)), dma((peers,)),
            dma((peers,)), dma((n // 2 - 1,)), dma((blocks,)), dma((blocks // 2,)),
        ],
        compiler_params=pltpu.CompilerParams(
            vmem_limit_bytes=VMEM_LIMIT, collective_id=1, has_side_effects=True
        ),
        name="merge",
    )(part, stat, seq, w_out, w_both)


def transition_kernel(
    pair_ref, left_ref, right_ref, w_outer_ref, bias_ref, w_up_ref, w_down_ref, out_ref,
    left_t, right_s, left_d, up_ref, down_ref, down_hi_ref,
):
    step = pl.program_id(0)
    group, cols, channels = pair_ref.shape
    proj = left_ref.shape[1]
    dot = functools.partial(jnp.dot, preferred_element_type=F32)

    @pl.when(step == 0)
    def _():
        left = left_ref[...]
        left_t[...] = left.T
        left_d[...] = jnp.dot(left, w_outer_ref[proj:], precision=HIGH) + bias_ref[...]
        r_hi, r_lo = halves(right_ref[...])
        right_s[...] = jnp.concatenate([r_hi, r_lo, r_hi], axis=1)
        up_hi, up_lo = halves(w_up_ref[...])
        up_ref[...] = jnp.concatenate([up_hi, up_hi, up_lo], axis=0)
        down_hi, down_lo = halves(w_down_ref[...])
        down_ref[...] = jnp.concatenate([down_hi, down_lo], axis=1)
        down_hi_ref[...] = down_hi

    lane = lax.broadcasted_iota(jnp.int32, left_t.shape, 1)
    w_prod = w_outer_ref[:proj]
    w_diff = w_outer_ref[proj:]
    weights = []
    for g in range(group):
        column = jnp.sum(
            jnp.where(lane == step * group + g, left_t[...], 0.0), axis=1, keepdims=True
        )
        w_hi, w_lo = halves(column * w_prod - w_diff)
        weights.append(jnp.concatenate([w_hi, w_hi, w_lo], axis=0))
    outer = dot(right_s[...], jnp.concatenate(weights, axis=1))
    for g in range(group):
        mid = pair_ref[g] + (
            outer[:, g * channels : (g + 1) * channels]
            + left_d[pl.ds(step * group + g, 1), :]
        )
        x_hi, x_lo = halves(channel_norm(mid))
        hidden = jnp.maximum(dot(jnp.concatenate([x_hi, x_lo, x_hi], axis=1), up_ref[...]), 0.0)
        h_hi, h_lo = halves(hidden)
        both = dot(h_hi, down_ref[...])
        out_ref[g] = mid + (
            both[:, :channels] + (both[:, channels:] + dot(h_lo, down_hi_ref[...]))
        )


def transition(pair, left, right, w_outer, outer_bias, w_up, w_down):
    rows, cols, channels = pair.shape
    proj = left.shape[1]
    hidden = w_up.shape[1]
    group = 4

    def whole(x):
        return pl.BlockSpec(x.shape, lambda i: (0,) * x.ndim)

    block = pl.BlockSpec((group, cols, channels), lambda i: (i, 0, 0))
    fixed = (left, right, w_outer, outer_bias.reshape(1, channels), w_up, w_down)
    return pl.pallas_call(
        transition_kernel,
        out_shape=jax.ShapeDtypeStruct(pair.shape, F32),
        grid=(rows // group,),
        in_specs=[block] + [whole(x) for x in fixed],
        out_specs=block,
        scratch_shapes=[
            pltpu.VMEM((proj, rows), F32),
            pltpu.VMEM((cols, 3 * proj), BF16),
            pltpu.VMEM((rows, channels), F32),
            pltpu.VMEM((3 * channels, hidden), BF16),
            pltpu.VMEM((hidden, 2 * channels), BF16),
            pltpu.VMEM((hidden, channels), BF16),
        ],
        compiler_params=pltpu.CompilerParams(vmem_limit_bytes=VMEM_LIMIT),
        name="transition",
    )(pair, *fixed)


def per_device(
    seq, query, key, value, pair, w_bias, w_out, w_left, w_right, w_outer, outer_bias, w_up, w_down
):
    rows, cols, channels = pair.shape
    heads = w_bias.shape[1]
    width = w_out.shape[0]
    head_dim = width // heads
    part, stat = gather_attention(query, key, value, pair, w_bias)
    seq_new, left, right = merge(
        part, stat, seq, w_out, w_left, w_right, head_dim, heads, cols
    )
    pair_new = transition(pair, left, right, w_outer, outer_bias, w_up, w_down)
    return seq_new, pair_new


def solution(mesh):
    in_specs = (
        P("row", "col"),
        P("row", "col"),
        P("col", "row"),
        P("col", "row"),
        P("row", "col", None),
        P(),
        P(None, "col"),
        P("col", None),
        P("col", None),
        P(),
        P(),
        P(),
        P(),
    )
    out_specs = (P("row", "col"), P("row", "col", None))
    return jax.shard_map(
        per_device, mesh=mesh, in_specs=in_specs, out_specs=out_specs, check_vma=False
    )
```

profile of v0, /device:TPU:0, one launch (start us, length us, event | category | flops | bytes accessed | tf_op | source)
XLA Modules:
  0.0 104.2 jit_solution(15495554719512928892)
XLA Ops:
  0.6 1.0 %reshape.26 = f32[48,4,2,64]{3,2,1,0:T(2,128)S(1)} reshape(f32[48,512]{1,0:T(8,128)} %param.14) | data formatting | bytes 196608 | tf_op jit(solution)/shard_map/reshape | solution.py:218
  1.8 0.1 pad_bitcast_fusion
  1.9 0.7 pad_maximum_fusion.1
  2.6 1.0 copy.15
  3.6 1.0 copy.16
  4.6 0.9 maximum_select_fusion.kv_ref
  5.5 1.0 copy.21
  6.5 1.0 copy.22
  7.5 0.8 pad_maximum_fusion.w_both_ref
  8.4 1.9 %fusion = (bf16[256,1024]{1,0:T(8,128)(2,1)}, bf16[256,1024]{1,0:T(8,128)(2,1)}) fusion(f32[8,8]{0,1:T(8,128)S(1)} %fusion.1, f32[32,128]{1,0:T(8,128)} %bitcast.21), kind=kLoop, calls=%fused_computation.2 | loop fusion | flops 1310720 | bytes 1065216 | tf_op jit(solution)/shard_map/convert_element_type | solution.py:25
  10.3 35.1 %gather_attention.1 = (f32[8,48,128]{2,1,0:T(8,128)}, f32[2,48,128]{2,1,0:T(8,128)}) custom-call(f32[384,128]{1,0:T(8,128)} %maximum_select_fusion.kv_ref, f32[8,48,128]{2,1,0:T(8,128)} %bitcast.20, f32[48,384,128]{2,1,0:T(8,128)} %pair_ref.3, bf16[256,1024]{1,0:T(8,128)(2,1)} %get-tuple-element.15.wt_hi_ref, bf16[256,1024]{1,0:T(8,128)(2,1)} %get-tuple-element.14.wt_lo_ref), custom_call_target="tpu_custom_call" | custom-call | tf_op jit(solution)/shard_map/gather_attention/pallas_call | solution.py:228
  45.4 26.2 %merge.1 = (f32[48,512]{1,0:T(8,128)}, f32[48,64]{1,0:T(8,128)}, f32[384,64]{1,0:T(8,128)}) custom-call(f32[8,48,128]{2,1,0:T(8,128)} %get-tuple-element.7.part_ref, f32[2,48,128]{2,1,0:T(8,128)} %get-tuple-element.8.stat_ref, f32[48,512]{1,0:T(8,128)} %seq_ref.1, f32[1024,512]{1,0:T(8,128)} %w_out_ref.1, f32[512,128]{1,0:T(8,128)} %pad_maximum_fusion.w_both_ref), custom_call_target="tpu_custom_call" | custom-call | tf_op jit(solution)/shard_map/merge/pallas_call | solution.py:407
  71.6 0.0 copy-start
  71.6 31.9 %transition.1 = f32[48,384,128]{2,1,0:T(8,128)} custom-call(f32[48,384,128]{2,1,0:T(8,128)} %pair_ref.3, f32[48,64]{1,0:T(8,128)} %get-tuple-element.10.left_ref, f32[384,64]{1,0:T(8,128)} %get-tuple-element.11.right_ref, f32[128,128]{1,0:T(8,128)} %w_outer_ref.1, f32[1,128]{1,0:T(1,128)} %bitcast.22, f32[128,512]{1,0:T(8,128)} %w_up_ref.1, ...), custom_call_target="tpu_custom_call" | custom-call | tf_op jit(solution)/shard_map/transition/pallas_call | solution.py:491
  103.5 0.0 copy-done
  103.5 0.6 copy.26
  (3 shorter events, 0.1 us)
Async XLA Ops:
  71.6 31.9 %copy-start = (f32[48,512]{1,0:T(8,128)S(1)}, f32[48,512]{1,0:T(8,128)}, u32[]{:S(2)}) copy-start(f32[48,512]{1,0:T(8,128)} %get-tuple-element.20) | copy-start | bytes 294916
where the time goes:
time: 105 us; the launch traced here: 104 us
  Pallas kernels  93.2 us (89%)
  local copies, waits for them, and re-layouts  5.94 us (6%)
  other arithmetic  4.35 us (4%)
    pallas_call x1, Pallas kernels, gather_attention(): pl.pallas_call(functools.partial(gather_attention_kernel, n, n_col, head_...  35.1 us
    pallas_call x1, Pallas kernels, transition(): pl.pallas_call(transition_kernel, out_shape=jax.ShapeDtypeStruct(pair.sha...  31.9 us
    pallas_call x1, Pallas kernels, merge(): pl.pallas_call(functools.partial(merge_kernel, n, n_col, head_dim, heads)...  26.2 us
    unnamed x7, local copies, waits for them, and re-layouts  4.74 us

commit v1 on v0

v1 whole, which is shorter than its diff:
```python
import functools

import jax
import jax.numpy as jnp
from jax import lax
from jax.experimental import pallas as pl
from jax.experimental.pallas import tpu as pltpu
from jax.sharding import PartitionSpec as P

HIGH = lax.Precision.HIGHEST
F32 = jnp.float32
BF16 = jnp.bfloat16
F8 = jnp.float8_e4m3fn
HIDDEN_SCALE = 2.0**11
DOWN_SCALE = 2.0**10
VMEM_LIMIT = 60 * 1024 * 1024
MESH = pl.DeviceIdType.MESH


def halves(x):
    high = x.astype(BF16)
    low = (x - high.astype(F32)).astype(BF16)
    return high, low


def channel_norm(x):
    centre = x - jnp.mean(x, axis=-1, keepdims=True)
    return centre * lax.rsqrt(jnp.mean(centre * centre, axis=-1, keepdims=True) + 1e-05)


def dot_nt(a, b, precision=None):
    return lax.dot_general(
        a, b, (((1,), (1,)), ((), ())), precision=precision, preferred_element_type=F32
    )


def split3(x):
    high = x.astype(BF16)
    rest = x - high.astype(F32)
    mid = rest.astype(BF16)
    low = (rest - mid.astype(F32)).astype(BF16)
    return high, mid, low


def sequence_kernel(
    n, n_col, head_dim, heads,
    kt_ref, vt_ref, q_ref, pair_ref, wbt_ref, seq_ref, w_out_ref, wlt_ref, wrt_ref,
    seq_out, left_out, right_out,
    k_buf, v_buf, q_buf, q_cat, bias_buf, pair_buf, rep_buf, wt_hi_ref, wt_lo_ref,
    w_out_buf, both_t, acc, msg, msg_in, sums, sums_in, packet, packet_in, right_mine, right_buf,
    recv_sem, z_sem, y_sem, core_sem, q_send, q_recv, pair_sem, load_sem,
    msg_send, msg_recv, sums_send, sums_recv, pack_send, pack_recv,
    right_send, right_recv, relay_send,
):
    n_z = n // 4
    feats, cols = kt_ref.shape
    rows, here = q_ref.shape
    width = w_out_ref.shape[0]
    proj = left_out.shape[1]
    groups, group = pair_buf.shape[:2]
    channels = pair_buf.shape[3]
    chip_heads = 2 * feats // head_dim
    wide = 2 * feats
    blocks = right_buf.shape[0]
    row, col = lax.axis_index("row"), lax.axis_index("col")
    core, y, z = lax.rem(row, 2), lax.rem(lax.div(row, 2), 2), lax.div(row, 4)
    core_peer, y_peer = row + 1 - 2 * core, row + 2 - 4 * y
    row_peers = [lax.rem(row + 2 * k, n) for k in range(1, n // 2)]
    col_peers = [lax.rem(col + k, n_col) for k in range(1, n_col)]
    signs = (1, -1)
    dot = functools.partial(jnp.dot, preferred_element_type=F32)

    def put(src, dst, send, recv, peer):
        return pltpu.make_async_remote_copy(
            src_ref=src, dst_ref=dst, send_sem=send, recv_sem=recv,
            device_id=peer, device_id_type=MESH,
        )

    def pair_copy(g):
        return pltpu.make_async_copy(
            pair_ref.at[pl.ds(g * group, group)], pair_buf.at[g], pair_sem.at[g]
        )

    bufs, owns = (k_buf, v_buf), (kt_ref, vt_ref)
    pair_copy(0).start()
    loads = [
        pltpu.make_async_copy(owns[kind], bufs[kind].at[row], recv_sem.at[row, kind])
        for kind in range(2)
    ]
    loads += [
        pltpu.make_async_copy(q_ref, q_buf.at[col], q_recv.at[col]),
        pltpu.make_async_copy(wlt_ref, both_t.at[:proj], load_sem.at[0]),
        pltpu.make_async_copy(wrt_ref, both_t.at[proj:], load_sem.at[1]),
        pltpu.make_async_copy(seq_ref, acc, load_sem.at[2]),
    ]
    for copy in loads:
        copy.start()
    for g in range(1, groups):
        pair_copy(g).start()
    load_w_out = pltpu.make_async_copy(w_out_ref, w_out_buf, load_sem.at[3])
    load_w_out.start()

    barrier = pltpu.get_barrier_semaphore()
    for peer in row_peers + [core_peer]:
        pl.semaphore_signal(barrier, inc=1, device_id={"row": peer}, device_id_type=MESH)
    for peer in col_peers:
        pl.semaphore_signal(barrier, inc=1, device_id={"col": peer}, device_id_type=MESH)
    pl.semaphore_wait(barrier, n // 2 + n_col - 1)

    def send_slot(src, kind, slot, sem, peer):
        return put(src, bufs[kind].at[slot], sem, recv_sem.at[slot, kind], {"row": peer})

    def inside(place):
        return jnp.logical_and(place >= 0, place < n_z)

    def own_sends(kind, act):
        for s, sign in enumerate(signs):

            @pl.when(inside(z + sign))
            def _():
                act(send_slot(owns[kind], kind, row, z_sem.at[0, s, kind], row + 4 * sign))

        act(send_slot(owns[kind], kind, row, y_sem.at[0, 0, kind], y_peer))
        act(send_slot(owns[kind], kind, row, core_sem.at[0, 0, 0, kind], core_peer))

    def line_sends(d, kind, act, wait):
        for s, sign in enumerate(signs):

            @pl.when(inside(z + sign * d))
            def _():
                slot = row + 4 * sign * d
                src = bufs[kind].at[slot]
                if wait:
                    send_slot(src, kind, slot, y_sem.at[d, s, kind], y_peer).wait_recv()

                @pl.when(inside(z - sign))
                def _():
                    act(send_slot(src, kind, slot, z_sem.at[d, s, kind], row - 4 * sign))

                act(send_slot(src, kind, slot, y_sem.at[d, s, kind], y_peer))
                act(send_slot(src, kind, slot, core_sem.at[d, s, 0, kind], core_peer))

    def cross_sends(d, kind, act, wait):
        for s, sign in enumerate(signs[: 1 if d == 0 else 2]):

            @pl.when(inside(z + sign * d))
            def _():
                slot = y_peer + 4 * sign * d
                src = bufs[kind].at[slot]
                copy = send_slot(src, kind, slot, core_sem.at[d, s, 1, kind], core_peer)
                if wait:
                    copy.wait_recv()
                act(copy)

    start = lambda copy: copy.start()
    wait_send = lambda copy: copy.wait_send()

    def q_copy(k, source):
        return put(
            q_ref, q_buf.at[source], q_send.at[k], q_recv.at[source], {"col": col_peers[k]}
        )

    own_sends(0, start)
    for k in range(n_col - 1):
        q_copy(k, col).start()
    own_sends(1, start)
    for copy in loads:
        copy.wait()

    both_hi, both_lo = halves(both_t[...])
    ones = jnp.ones((8, here), BF16)
    sums[...] = dot_nt(ones, both_hi) + dot_nt(ones, both_lo)
    sum_copies = [
        put(sums, sums_in.at[k], sums_send.at[k], sums_recv.at[k], {"col": peer})
        for k, peer in enumerate(col_peers)
    ]

    for h in range(heads):
        rep_buf[h * group : (h + 1) * group] = jnp.broadcast_to(
            wbt_ref[h : h + 1, :], (group, channels)
        )
    place = lax.rem(lax.broadcasted_iota(jnp.int32, rep_buf.shape, 0), group)
    for i in range(group):
        high, low = halves(jnp.where(place == i, rep_buf[...], 0.0))
        wt_hi_ref[:, i * channels : (i + 1) * channels] = high
        wt_lo_ref[:, i * channels : (i + 1) * channels] = low
    for copy in sum_copies:
        copy.start()

    def bias_group(g, carry):
        pair_copy(g).wait()
        parts = [halves(channel_norm(pair_buf[g, i])) for i in range(group)]
        high = jnp.concatenate([p[0] for p in parts], axis=1)
        low = jnp.concatenate([p[1] for p in parts], axis=1)
        wt_hi = wt_hi_ref[...]
        flat = dot_nt(wt_hi, high) + (dot_nt(wt_hi, low) + dot_nt(wt_lo_ref[...], high))
        bias_buf[:, pl.ds(pl.multiple_of(g * group, group), group), :] = flat.reshape(
            heads, group, flat.shape[1]
        )
        return carry

    def bias_groups(part):
        lax.fori_loop(part * groups // 3, (part + 1) * groups // 3, bias_group, 0)

    tile = 128
    tile_heads = tile // head_dim
    per_col = here // tile
    scale = F32(head_dim) ** -0.5

    def spread_queries(index, carry):
        at = pl.multiple_of(lax.rem(index, per_col) * tile, tile)
        q = q_buf[lax.div(index, per_col), :, pl.ds(at, tile)] * scale
        turns = [q] + [pltpu.roll(q, m * head_dim, 1) for m in range(1, tile_heads)]
        lane = lax.broadcasted_iota(jnp.int32, q.shape, 1) // head_dim
        for m in range(tile_heads):
            every = turns[(0 - m) % tile_heads]
            for p in range(1, tile_heads):
                every = jnp.where(lane == p, turns[(p - m) % tile_heads], every)
            high, mid, low = [part.astype(F32) for part in split3(every)]
            first = jnp.where(lane == 2, mid, high).astype(BF16)
            second = jnp.where(lane == 0, mid, low).astype(BF16)
            q_cat[index * tile_heads + m] = jnp.concatenate(
                [first, second[:, : 2 * head_dim]], axis=1
            )
        return carry

    def event(d, kind):
        line_sends(d, kind, start, True)
        cross_sends(d - 1, kind, start, True)

    lane = lax.broadcasted_iota(jnp.int32, (rows, wide), 1)
    head_lane = lane // head_dim
    upper = lax.rem(lane, head_dim) >= head_dim // 2

    def msg_copies(chip):
        return [
            put(
                msg.at[chip], msg_in.at[k, chip], msg_send.at[k, chip], msg_recv.at[k, chip],
                {"col": peer},
            )
            for k, peer in enumerate(col_peers)
        ]

    def order(t):
        out = jnp.int32(0)
        for here_z in range(n_z):
            up_first = here_z < n_z - 1 - here_z
            ranked = sorted(
                range(n_z),
                key=lambda a: (abs(a - here_z), (a < here_z) if up_first else (a > here_z)),
            )
            out = out + ranked[t] * (z == here_z).astype(jnp.int32)
        return out

    def chip_at(t, u):
        return 2 * order(t) + y + u * (1 - 2 * y)

    def attend(t, u):
        chip = chip_at(t, u)
        base = 2 * chip
        other = base + 1 - core
        for kind in range(2):
            put(
                bufs[kind].at[other], bufs[kind].at[other], core_sem.at[0, 0, 0, kind],
                recv_sem.at[other, kind], {"row": core_peer},
            ).wait_recv()
        keys = k_buf[pl.ds(base, 2)].reshape(wide, cols)
        values = v_buf[pl.ds(base, 2)].reshape(wide, cols)
        k_hi, k_mid, k_lo = split3(keys)
        expos, part_stat = [], jnp.zeros((rows, wide), F32)
        for m in range(chip_heads):
            mine = slice(m * head_dim, (m + 1) * head_dim)
            a, b, c = k_hi[mine], k_mid[mine], k_lo[mine]
            head = chip * chip_heads + m
            stacked = jnp.concatenate([a, b, a, c, b, a], axis=0)
            scores = dot(q_cat[head], stacked) + bias_buf[head]
            top = jnp.max(scores, axis=1, keepdims=True)
            expo = jnp.exp(scores - top)
            total = jnp.sum(expo, axis=1, keepdims=True)
            expos.append(expo)
            part_stat = jnp.where(head_lane == m, jnp.where(upper, total, top), part_stat)
        e_hi, e_lo = halves(jnp.concatenate(expos, axis=0))
        v_hi, v_lo = halves(values)
        out = dot_nt(e_hi, v_hi) + (dot_nt(e_hi, v_lo) + dot_nt(e_lo, v_hi))
        part = out[:rows]
        for m in range(1, chip_heads):
            part = jnp.where(head_lane == m, out[m * rows : (m + 1) * rows], part)
        msg[chip, :rows] = part
        msg[chip, rows:] = part_stat
        for copy in msg_copies(chip):
            copy.start()

    def combine(t, u):
        chip = chip_at(t, u)
        for copy in msg_copies(chip):
            copy.wait()
        every = [msg[chip]] + [msg_in[k, chip] for k in range(n_col - 1)]
        stats = [e[rows:] for e in every]
        down = [pltpu.roll(s, wide - head_dim // 2, 1) for s in stats]
        up = [pltpu.roll(s, head_dim // 2, 1) for s in stats]
        tops = [jnp.where(upper, r, s) for s, r in zip(stats, up)]
        totals = [jnp.where(upper, s, r) for s, r in zip(stats, down)]
        highest = functools.reduce(jnp.maximum, tops)
        scales = [jnp.exp(top - highest) for top in tops]
        total = sum(s * t for s, t in zip(scales, totals))
        attn = sum(e[:rows] * s for e, s in zip(every, scales)) / total
        a_hi, a_lo = halves(attn)
        at = pl.multiple_of(chip * wide, wide)
        w_hi, w_lo = halves(w_out_buf[pl.ds(at, wide), :])
        acc[...] += dot(a_hi, w_hi) + (dot(a_hi, w_lo) + dot(a_lo, w_hi))

    def stage(t):
        def one(u, carry):
            attend(t, u)
            if t:
                combine(t - 1, u)
            return carry

        lax.fori_loop(0, 2, one, 0)

    bias_groups(0)
    event(1, 0)
    bias_groups(1)
    event(1, 1)
    bias_groups(2)
    for k in range(1, n_col):
        source = lax.rem(col - k + n_col, n_col)
        q_copy(k - 1, source).wait_recv()
    lax.fori_loop(0, heads // tile_heads, spread_queries, 0)
    load_w_out.wait()
    for d in range(2, n_z):
        event(d, 0)
        stage(d - 2)
        event(d, 1)
    stage(n_z - 2)
    attend(n_z - 1, 0)
    combine(n_z - 2, 0)
    for kind in range(2):
        cross_sends(n_z - 1, kind, start, True)
    attend(n_z - 1, 1)
    combine(n_z - 2, 1)
    for copy in sum_copies:
        copy.wait()
    for u in range(2):
        combine(n_z - 1, u)

    seq_new = acc[...]
    seq_out[...] = seq_new
    local_mean = jnp.mean(seq_new, axis=1, keepdims=True)
    centred = seq_new - local_mean
    spread = jnp.sum(centred * centred, axis=1, keepdims=True)
    both_hi, both_lo = halves(both_t[...])
    c_hi, c_lo = halves(centred)
    packet[:rows] = dot_nt(c_hi, both_hi) + (dot_nt(c_hi, both_lo) + dot_nt(c_lo, both_hi))
    wide_lane = lax.broadcasted_iota(jnp.int32, (rows, 2 * proj), 1)
    packet[rows:] = jnp.where(wide_lane < proj, local_mean, spread)
    packets = [
        put(packet, packet_in.at[k], pack_send.at[k], pack_recv.at[k], {"col": peer})
        for k, peer in enumerate(col_peers)
    ]
    for copy in packets:
        copy.start()
    for copy in packets:
        copy.wait()
    every = [packet[...]] + [packet_in[k] for k in range(n_col - 1)]
    weights = [sums[:1]] + [sums_in[k, :1] for k in range(n_col - 1)]
    means = [p[rows:, :1] for p in every]
    mean = sum(means) / n_col
    offsets = [m - mean for m in means]
    variance = (
        sum(p[rows:, proj : proj + 1] for p in every) + here * sum(o * o for o in offsets)
    ) / width
    both = sum(p[:rows] + o * w for p, o, w in zip(every, offsets, weights))
    both = both * lax.rsqrt(variance + 1e-05)
    left_out[...] = both[:, :proj]
    half = rows // 2
    right_mine[...] = jnp.concatenate([both[:half, proj:], both[half:, proj:]], axis=1)

    mine = lax.div(row, blocks) == col
    own = lax.rem(row, blocks)

    def row_copies():
        return [
            put(
                right_mine, right_buf.at[own], right_send.at[k], right_recv.at[own],
                {"row": peer},
            )
            for k, peer in enumerate(row_peers)
        ]

    @pl.when(mine)
    def _():
        for copy in row_copies():
            copy.start()
        keep = pltpu.make_async_copy(right_mine, right_buf.at[own], right_recv.at[own])
        keep.start()
        keep.wait()

    def relay(j, block):
        slot = right_buf.at[block]
        return put(slot, slot, relay_send.at[j], right_recv.at[block], {"row": core_peer})

    for j in range(blocks // 2):
        block = 2 * j + core

        @pl.when(col * blocks + block != row)
        def _():
            relay(j, block).wait_recv()

        relay(j, block).start()
    for j in range(blocks // 2):
        relay(j, 2 * j + 1 - core).wait_recv()
    for b in range(blocks):
        packed = right_buf[b]
        right_out[b * rows : b * rows + half] = packed[:, :proj]
        right_out[b * rows + half : (b + 1) * rows] = packed[:, proj:]

    for j in range(blocks // 2):
        relay(j, 2 * j + core).wait_send()

    @pl.when(mine)
    def _():
        for copy in row_copies():
            copy.wait_send()

    for kind in range(2):
        own_sends(kind, wait_send)
        for d in range(1, n_z):
            line_sends(d, kind, wait_send, False)
        for d in range(n_z):
            cross_sends(d, kind, wait_send, False)
    for k in range(n_col - 1):
        q_copy(k, col).wait_send()


def sequence_update(seq, query, key, value, pair, w_bias, w_out, w_left, w_right):
    n, n_col = lax.axis_size("row"), lax.axis_size("col")
    rows, cols, channels = pair.shape
    heads = w_bias.shape[1]
    feats = key.shape[1]
    width, here = w_out.shape
    head_dim = width // heads
    proj = w_left.shape[1]
    blocks = cols // rows
    group = 8
    peers = n_col - 1
    n_z = n // 4
    chips = n // 2
    any_space = pl.BlockSpec(memory_space=pl.ANY)
    vmem = pl.BlockSpec(memory_space=pltpu.VMEM)
    dma = pltpu.SemaphoreType.DMA
    return pl.pallas_call(
        functools.partial(sequence_kernel, n, n_col, head_dim, heads),
        out_shape=(
            jax.ShapeDtypeStruct(seq.shape, F32),
            jax.ShapeDtypeStruct((rows, proj), F32),
            jax.ShapeDtypeStruct((cols, proj), F32),
        ),
        in_specs=[any_space] * 4 + [vmem] + [any_space] * 4,
        out_specs=(vmem,) * 3,
        scratch_shapes=[
            pltpu.VMEM((n, feats, cols), F32),
            pltpu.VMEM((n, feats, cols), F32),
            pltpu.VMEM((n_col, rows, here), F32),
            pltpu.VMEM((heads, rows, 6 * head_dim), BF16),
            pltpu.VMEM((heads, rows, cols), F32),
            pltpu.VMEM((rows // group, group, cols, channels), F32),
            pltpu.VMEM((heads * group, channels), F32),
            pltpu.VMEM((heads * group, group * channels), BF16),
            pltpu.VMEM((heads * group, group * channels), BF16),
            pltpu.VMEM((width, here), F32),
            pltpu.VMEM((2 * proj, here), F32),
            pltpu.VMEM((rows, here), F32),
            pltpu.VMEM((chips, 2 * rows, 2 * feats), F32),
            pltpu.VMEM((peers, chips, 2 * rows, 2 * feats), F32),
            pltpu.VMEM((8, 2 * proj), F32),
            pltpu.VMEM((peers, 8, 2 * proj), F32),
            pltpu.VMEM((2 * rows, 2 * proj), F32),
            pltpu.VMEM((peers, 2 * rows, 2 * proj), F32),
            pltpu.VMEM((rows // 2, 2 * proj), F32),
            pltpu.VMEM((blocks, rows // 2, 2 * proj), F32),
            dma((n, 2)), dma((n_z, 2, 2)), dma((n_z, 2, 2)), dma((n_z, 2, 2, 2)),
            dma((peers,)), dma((n_col,)), dma((rows // group,)), dma((4,)),
            dma((peers, chips)), dma((peers, chips)), dma((peers,)), dma((peers,)),
            dma((peers,)), dma((peers,)),
            dma((n // 2 - 1,)), dma((blocks,)), dma((blocks // 2,)),
        ],
        compiler_params=pltpu.CompilerParams(
            vmem_limit_bytes=VMEM_LIMIT, collective_id=0, has_side_effects=True
        ),
        name="sequence_update",
    )(key.T, value.T, query, pair, w_bias.T, seq, w_out, w_left.T, w_right.T)


def transition_kernel(
    pair_ref, left_ref, right_ref, w_outer_ref, bias_ref, w_up_ref, w_down_ref, seq_ref,
    seq_out, out_ref,
    left_t, right_s, left_d, up_ref, up8_ref, down_ref, down8_ref,
):
    step = pl.program_id(0)
    group, cols, channels = pair_ref.shape
    proj = left_ref.shape[1]
    dot = functools.partial(jnp.dot, preferred_element_type=F32)

    @pl.when(step == 0)
    def _():
        seq_out[...] = seq_ref[...]
        left = left_ref[...]
        left_t[...] = left.T
        left_d[...] = jnp.dot(left, w_outer_ref[proj:], precision=HIGH) + bias_ref[...]
        r_hi, r_lo = halves(right_ref[...])
        right_s[...] = jnp.concatenate([r_hi, r_lo, r_hi], axis=1)
        up = w_up_ref[...] * HIDDEN_SCALE
        up_hi = up.astype(BF16)
        up_ref[...] = jnp.concatenate([up_hi, up_hi], axis=0)
        up8_ref[...] = (up - up_hi.astype(F32)).astype(F8)
        down = w_down_ref[...] * (1.0 / HIDDEN_SCALE)
        down_hi, down_lo = halves(down)
        down_ref[...] = jnp.concatenate([down_hi, down_lo], axis=1)
        down8_ref[...] = (w_down_ref[...] * DOWN_SCALE).astype(F8)

    lane = lax.broadcasted_iota(jnp.int32, left_t.shape, 1)
    w_prod = w_outer_ref[:proj]
    w_diff = w_outer_ref[proj:]
    weights = []
    for g in range(group):
        column = jnp.sum(
            jnp.where(lane == step * group + g, left_t[...], 0.0), axis=1, keepdims=True
        )
        w_hi, w_lo = halves(column * w_prod - w_diff)
        weights.append(jnp.concatenate([w_hi, w_hi, w_lo], axis=0))
    outer = dot(right_s[...], jnp.concatenate(weights, axis=1))
    for first in range(0, group, 2):
        pick = range(first, first + 2)
        mids = [
            pair_ref[g]
            + (
                outer[:, g * channels : (g + 1) * channels]
                + left_d[pl.ds(step * group + g, 1), :]
            )
            for g in pick
        ]
        xs = [channel_norm(mid) for mid in mids]
        pairs = [jnp.concatenate(halves(x), axis=1) for x in xs]
        main = [dot(x, up_ref[...]) for x in pairs]
        rest = [dot(x.astype(F8), up8_ref[...]) for x in xs]
        hidden = [jnp.maximum(m + r, 0.0) for m, r in zip(main, rest)]
        highs = [h.astype(BF16) for h in hidden]
        lows = [(h - high.astype(F32)).astype(F8) for h, high in zip(hidden, highs)]
        both = [dot(high, down_ref[...]) for high in highs]
        rest = [dot(low, down8_ref[...]) * (1.0 / (HIDDEN_SCALE * DOWN_SCALE)) for low in lows]
        for g, mid, b, r in zip(pick, mids, both, rest):
            out_ref[g] = mid + (b[:, :channels] + (b[:, channels:] + r))


def transition(pair, left, right, w_outer, outer_bias, w_up, w_down, seq_new):
    rows, cols, channels = pair.shape
    proj = left.shape[1]
    hidden = w_up.shape[1]
    group = 4

    def whole(x):
        return pl.BlockSpec(x.shape, lambda i: (0,) * x.ndim)

    block = pl.BlockSpec((group, cols, channels), lambda i: (i, 0, 0))
    fixed = (left, right, w_outer, outer_bias.reshape(1, channels), w_up, w_down, seq_new)
    return pl.pallas_call(
        transition_kernel,
        out_shape=(
            jax.ShapeDtypeStruct(seq_new.shape, F32),
            jax.ShapeDtypeStruct(pair.shape, F32),
        ),
        grid=(rows // group,),
        in_specs=[block] + [whole(x) for x in fixed],
        out_specs=(whole(seq_new), block),
        scratch_shapes=[
            pltpu.VMEM((proj, rows), F32),
            pltpu.VMEM((cols, 3 * proj), BF16),
            pltpu.VMEM((rows, channels), F32),
            pltpu.VMEM((2 * channels, hidden), BF16),
            pltpu.VMEM((channels, hidden), F8),
            pltpu.VMEM((hidden, 2 * channels), BF16),
            pltpu.VMEM((hidden, channels), F8),
        ],
        compiler_params=pltpu.CompilerParams(vmem_limit_bytes=VMEM_LIMIT),
        name="transition",
    )(pair, *fixed)


def per_device(
    seq, query, key, value, pair, w_bias, w_out, w_left, w_right, w_outer, outer_bias, w_up, w_down
):
    seq_new, left, right = sequence_update(
        seq, query, key, value, pair, w_bias, w_out, w_left, w_right
    )
    return transition(pair, left, right, w_outer, outer_bias, w_up, w_down, seq_new)


def solution(mesh):
    in_specs = (
        P("row", "col"),
        P("row", "col"),
        P("col", "row"),
        P("col", "row"),
        P("row", "col", None),
        P(),
        P(None, "col"),
        P("col", None),
        P("col", None),
        P(),
        P(),
        P(),
        P(),
    )
    out_specs = (P("row", "col"), P("row", "col", None))
    return jax.shard_map(
        per_device, mesh=mesh, in_specs=in_specs, out_specs=out_specs, check_vma=False
    )
```

time: 105 us -> 72.8 us (0.69)
  Pallas kernels: 93.2 us -> 71.9 us
  local copies, waits for them, and re-layouts: 5.94 us -> 0 us
  other arithmetic: 4.35 us -> 0 us
    pallas_call x3 -> x2, Pallas kernels: 93.2 us -> 71.9 us  [the longest x1 44.6 us: sequence_update(): pl.pallas_call(functools.partial(sequence_kernel, n, n_col, head_dim, hea...]
    unnamed x7 -> x0, local copies, waits for them, and re-layouts: 4.74 us -> none
    convert_element_type x2 -> x0, other arithmetic: 1.95 us -> none  [the longest x1 1.95 us: split(): return (kept.astype(BF16), (x - kept).astype(BF16))]
    reshape x2 -> x0, local copies, waits for them, and re-layouts: 1.09 us -> none  [gather_attention(): q = query.reshape(rows, n_slot // 2, 2, feats).transpose(1, 2, 0, 3)]
where the time goes in v1:
time: 72.8 us; the launch traced here: 72.5 us
  Pallas kernels  71.9 us (99%)
    pallas_call x1, Pallas kernels, sequence_update(): pl.pallas_call(functools.partial(sequence_kernel, n, n_col, head_dim, hea...  44.6 us
    pallas_call x1, Pallas kernels, transition(): pl.pallas_call(transition_kernel, out_shape=(jax.ShapeDtypeStruct(seq_new...  27.3 us

profile of v1, /device:TPU:0, one launch (start us, length us, event | category | flops | bytes accessed | tf_op | source)
XLA Modules:
  0.0 72.5 jit_solution(4943679974270203610)
XLA Ops:
  0.6 44.6 %sequence_update.1 = (f32[48,512]{1,0:T(8,128)}, f32[48,64]{1,0:T(8,128)}, f32[384,64]{1,0:T(8,128)}) custom-call(f32[64,384]{1,0:T(8,128)} %bitcast.8, f32[64,384]{1,0:T(8,128)} %bitcast.9, f32[48,512]{1,0:T(8,128)} %q_ref.1, f32[48,384,128]{2,1,0:T(8,128)} %pair_ref.3, f32[32,128]{1,0:T(8,128)} %bitcast.10, f32[48,512]{1,0:T(8,128)} %seq_ref.1, ...), custom_call_target="tpu_custom_call" | custom-call | tf_op jit(solution)/shard_map/sequence_update/pallas_call | solution.py:452
  45.2 27.3 %transition.1 = (f32[48,512]{1,0:T(8,128)}, f32[48,384,128]{2,1,0:T(8,128)}) custom-call(f32[48,384,128]{2,1,0:T(8,128)} %pair_ref.3, f32[48,64]{1,0:T(8,128)} %get-tuple-element.5.left_ref, f32[384,64]{1,0:T(8,128)} %get-tuple-element.6.right_ref, f32[128,128]{1,0:T(8,128)} %w_outer_ref.1, f32[1,128]{1,0:T(1,128)} %bitcast.11, f32[128,512]{1,0:T(8,128)} %w_up_ref.1, ...), custom_call_target="tpu_custom_call" | custom-call | tf_op jit(solution)/shard_map/transition/pallas_call | solution.py:567

commit v2 on v1

--- a/solution.py
+++ b/solution.py
@@ -14,6 +14,7 @@
 HIDDEN_SCALE = 2.0**11
 DOWN_SCALE = 2.0**10
 VMEM_LIMIT = 60 * 1024 * 1024
+LANES = 128
 MESH = pl.DeviceIdType.MESH
 
 
@@ -46,9 +47,9 @@
     n, n_col, head_dim, heads,
     kt_ref, vt_ref, q_ref, pair_ref, wbt_ref, seq_ref, w_out_ref, wlt_ref, wrt_ref,
     seq_out, left_out, right_out,
-    k_buf, v_buf, q_buf, q_cat, bias_buf, pair_buf, rep_buf, wt_hi_ref, wt_lo_ref,
+    k_buf, v_buf, q_buf, q_cat, bias_buf, pair_buf, wt_ref,
     w_out_buf, both_t, acc, msg, msg_in, sums, sums_in, packet, packet_in, right_mine, right_buf,
-    recv_sem, z_sem, y_sem, core_sem, q_send, q_recv, pair_sem, load_sem,
+    recv_sem, z_sem, y_sem, core_sem, around_sem, q_send, q_recv, pair_sem, load_sem,
     msg_send, msg_recv, sums_send, sums_recv, pack_send, pack_recv,
     right_send, right_recv, relay_send,
 ):
@@ -62,6 +63,7 @@
     chip_heads = 2 * feats // head_dim
     wide = 2 * feats
     blocks = right_buf.shape[0]
+    bias_tiles = bias_buf.shape[0]
     row, col = lax.axis_index("row"), lax.axis_index("col")
     core, y, z = lax.rem(row, 2), lax.rem(lax.div(row, 2), 2), lax.div(row, 4)
     core_peer, y_peer = row + 1 - 2 * core, row + 2 - 4 * y
@@ -81,8 +83,26 @@
             pair_ref.at[pl.ds(g * group, group)], pair_buf.at[g], pair_sem.at[g]
         )
 
+    def inside(place):
+        return jnp.logical_and(place >= 0, place < n_z)
+
+    barrier = pltpu.get_barrier_semaphore()
+
+    def greet(peer):
+        pl.semaphore_signal(barrier, inc=1, device_id=peer, device_id_type=MESH)
+
+    for sign in signs:
+
+        @pl.when(inside(z + sign))
+        def _():
+            greet({"row": row + 4 * sign})
+
+    for peer in (y_peer, core_peer):
+        greet({"row": peer})
+    for peer in col_peers:
+        greet({"col": peer})
+
     bufs, owns = (k_buf, v_buf), (kt_ref, vt_ref)
-    pair_copy(0).start()
     loads = [
         pltpu.make_async_copy(owns[kind], bufs[kind].at[row], recv_sem.at[row, kind])
         for kind in range(2)
@@ -95,33 +115,24 @@
     ]
     for copy in loads:
         copy.start()
-    for g in range(1, groups):
-        pair_copy(g).start()
-    load_w_out = pltpu.make_async_copy(w_out_ref, w_out_buf, load_sem.at[3])
-    load_w_out.start()
-
-    barrier = pltpu.get_barrier_semaphore()
-    for peer in row_peers + [core_peer]:
-        pl.semaphore_signal(barrier, inc=1, device_id={"row": peer}, device_id_type=MESH)
-    for peer in col_peers:
-        pl.semaphore_signal(barrier, inc=1, device_id={"col": peer}, device_id_type=MESH)
-    pl.semaphore_wait(barrier, n // 2 + n_col - 1)
+    neighbours = sum(inside(z + sign).astype(jnp.int32) for sign in signs)
+    pl.semaphore_wait(barrier, neighbours + 2 + len(col_peers))
 
     def send_slot(src, kind, slot, sem, peer):
         return put(src, bufs[kind].at[slot], sem, recv_sem.at[slot, kind], {"row": peer})
 
-    def inside(place):
-        return jnp.logical_and(place >= 0, place < n_z)
+    def at_end(place):
+        return place < -99
 
     def own_sends(kind, act):
         for s, sign in enumerate(signs):
 
             @pl.when(inside(z + sign))
             def _():
-                act(send_slot(owns[kind], kind, row, z_sem.at[0, s, kind], row + 4 * sign))
-
-        act(send_slot(owns[kind], kind, row, y_sem.at[0, 0, kind], y_peer))
-        act(send_slot(owns[kind], kind, row, core_sem.at[0, 0, 0, kind], core_peer))
+                act(send_slot(bufs[kind].at[row], kind, row, z_sem.at[0, s, kind], row + 4 * sign))
+
+        act(send_slot(bufs[kind].at[row], kind, row, y_sem.at[0, 0, kind], y_peer))
+        act(send_slot(bufs[kind].at[row], kind, row, core_sem.at[0, 0, 0, kind], core_peer))
 
     def line_sends(d, kind, act, wait):
         for s, sign in enumerate(signs):
@@ -137,13 +148,24 @@
                 def _():
                     act(send_slot(src, kind, slot, z_sem.at[d, s, kind], row - 4 * sign))
 
-                act(send_slot(src, kind, slot, y_sem.at[d, s, kind], y_peer))
+                if kind == 0:
+                    act(send_slot(src, kind, slot, y_sem.at[d, s, kind], y_peer))
+                else:
+
+                    @pl.when(jnp.logical_not(at_end(z + sign * d)))
+                    def _():
+                        act(send_slot(src, kind, slot, y_sem.at[d, s, kind], y_peer))
+
                 act(send_slot(src, kind, slot, core_sem.at[d, s, 0, kind], core_peer))
 
     def cross_sends(d, kind, act, wait):
         for s, sign in enumerate(signs[: 1 if d == 0 else 2]):
-
-            @pl.when(inside(z + sign * d))
+            source = z + sign * d
+            by_y = inside(source)
+            if kind and d:
+                by_y = jnp.logical_and(by_y, jnp.logical_not(at_end(source)))
+
+            @pl.when(by_y)
             def _():
                 slot = y_peer + 4 * sign * d
                 src = bufs[kind].at[slot]
@@ -152,6 +174,26 @@
                     copy.wait_recv()
                 act(copy)
 
+    def around_sends(d, act, wait):
+        for s, sign in enumerate(signs):
+            source = z + sign * d
+
+            @pl.when(jnp.logical_and(inside(source), at_end(source)))
+            def _():
+                slot = y_peer + 4 * sign * d
+                src = v_buf.at[slot]
+                if d:
+                    copy = send_slot(src, 1, slot, core_sem.at[d, s, 1, 1], core_peer)
+                    if wait:
+                        copy.wait_recv()
+
+                @pl.when(inside(z - sign))
+                def _():
+                    act(send_slot(src, 1, slot, around_sem.at[d, s], row - 4 * sign))
+
+                if d:
+                    act(copy)
+
     start = lambda copy: copy.start()
     wait_send = lambda copy: copy.wait_send()
 
@@ -160,11 +202,17 @@
             q_ref, q_buf.at[source], q_send.at[k], q_recv.at[source], {"col": col_peers[k]}
         )
 
+    loads[0].wait()
     own_sends(0, start)
     for k in range(n_col - 1):
         q_copy(k, col).start()
+    loads[1].wait()
     own_sends(1, start)
-    for copy in loads:
+    for g in range(groups):
+        pair_copy(g).start()
+    load_w_out = pltpu.make_async_copy(w_out_ref, w_out_buf, load_sem.at[3])
+    load_w_out.start()
+    for copy in loads[2:]:
         copy.wait()
 
     both_hi, both_lo = halves(both_t[...])
@@ -175,32 +223,26 @@
         for k, peer in enumerate(col_peers)
     ]
 
-    for h in range(heads):
-        rep_buf[h * group : (h + 1) * group] = jnp.broadcast_to(
-            wbt_ref[h : h + 1, :], (group, channels)
-        )
-    place = lax.rem(lax.broadcasted_iota(jnp.int32, rep_buf.shape, 0), group)
-    for i in range(group):
-        high, low = halves(jnp.where(place == i, rep_buf[...], 0.0))
-        wt_hi_ref[:, i * channels : (i + 1) * channels] = high
-        wt_lo_ref[:, i * channels : (i + 1) * channels] = low
+    wb_hi, wb_lo = halves(wbt_ref[...])
+    wt_ref[:heads] = jnp.concatenate([wb_hi, wb_hi], axis=1)
+    wt_ref[heads:] = jnp.concatenate([wb_lo, jnp.zeros_like(wb_lo)], axis=1)
     for copy in sum_copies:
         copy.start()
 
     def bias_group(g, carry):
         pair_copy(g).wait()
-        parts = [halves(channel_norm(pair_buf[g, i])) for i in range(group)]
-        high = jnp.concatenate([p[0] for p in parts], axis=1)
-        low = jnp.concatenate([p[1] for p in parts], axis=1)
-        wt_hi = wt_hi_ref[...]
-        flat = dot_nt(wt_hi, high) + (dot_nt(wt_hi, low) + dot_nt(wt_lo_ref[...], high))
-        bias_buf[:, pl.ds(pl.multiple_of(g * group, group), group), :] = flat.reshape(
-            heads, group, flat.shape[1]
-        )
+        for i in range(group):
+            x = jnp.concatenate(halves(channel_norm(pair_buf[g, i])), axis=1)
+            flat = dot_nt(wt_ref[...], x)
+            flat = flat[:heads] + flat[heads:]
+            if bias_tiles * LANES > cols:
+                spare = jnp.zeros((heads, bias_tiles * LANES - cols), F32)
+                flat = jnp.concatenate([flat, spare], axis=1)
+            for j in range(bias_tiles):
+                bias_buf[j, pl.ds(g * group + i, heads, stride=rows), :] = flat[
+                    :, j * LANES : (j + 1) * LANES
+                ]
         return carry
-
-    def bias_groups(part):
-        lax.fori_loop(part * groups // 3, (part + 1) * groups // 3, bias_group, 0)
 
     tile = 128
     tile_heads = tile // head_dim
@@ -226,17 +268,22 @@
 
     def event(d, kind):
         line_sends(d, kind, start, True)
+        if kind == 0 and d > 1:
+            around_sends(d - 1, start, True)
         cross_sends(d - 1, kind, start, True)
+        if kind and d == 1:
+            around_sends(0, start, True)
 
     lane = lax.broadcasted_iota(jnp.int32, (rows, wide), 1)
     head_lane = lane // head_dim
     upper = lax.rem(lane, head_dim) >= head_dim // 2
 
-    def msg_copies(chip):
+    def msg_copies(chip, part):
+        at = pl.ds(part * rows, rows)
         return [
             put(
-                msg.at[chip], msg_in.at[k, chip], msg_send.at[k, chip], msg_recv.at[k, chip],
-                {"col": peer},
+                msg.at[chip, at], msg_in.at[k, chip, at],
+                msg_send.at[k, chip, part], msg_recv.at[k, chip, part], {"col": peer},
             )
             for k, peer in enumerate(col_peers)
         ]
@@ -255,44 +302,59 @@
     def chip_at(t, u):
         return 2 * order(t) + y + u * (1 - 2 * y)
 
-    def attend(t, u):
+    def bias_of(head):
+        at = pl.ds(pl.multiple_of(head * rows, 8), rows)
+        tiles = [bias_buf[j, at, :] for j in range(bias_tiles)]
+        return jnp.concatenate(tiles, axis=1)[:, :cols]
+
+    def await_other(chip, kind):
+        other = 2 * chip + 1 - core
+        put(
+            bufs[kind].at[other], bufs[kind].at[other], core_sem.at[0, 0, 0, kind],
+            recv_sem.at[other, kind], {"row": core_peer},
+        ).wait_recv()
+
+    def attend_keys(t, u):
         chip = chip_at(t, u)
-        base = 2 * chip
-        other = base + 1 - core
-        for kind in range(2):
-            put(
-                bufs[kind].at[other], bufs[kind].at[other], core_sem.at[0, 0, 0, kind],
-                recv_sem.at[other, kind], {"row": core_peer},
-            ).wait_recv()
-        keys = k_buf[pl.ds(base, 2)].reshape(wide, cols)
-        values = v_buf[pl.ds(base, 2)].reshape(wide, cols)
+        await_other(chip, 0)
+        keys = k_buf[pl.ds(2 * chip, 2)].reshape(wide, cols)
         k_hi, k_mid, k_lo = split3(keys)
-        expos, part_stat = [], jnp.zeros((rows, wide), F32)
+        expos, stat = [], jnp.zeros((rows, wide), F32)
         for m in range(chip_heads):
             mine = slice(m * head_dim, (m + 1) * head_dim)
             a, b, c = k_hi[mine], k_mid[mine], k_lo[mine]
             head = chip * chip_heads + m
             stacked = jnp.concatenate([a, b, a, c, b, a], axis=0)
-            scores = dot(q_cat[head], stacked) + bias_buf[head]
+            scores = dot(q_cat[head], stacked) + bias_of(head)
             top = jnp.max(scores, axis=1, keepdims=True)
             expo = jnp.exp(scores - top)
             total = jnp.sum(expo, axis=1, keepdims=True)
             expos.append(expo)
-            part_stat = jnp.where(head_lane == m, jnp.where(upper, total, top), part_stat)
-        e_hi, e_lo = halves(jnp.concatenate(expos, axis=0))
-        v_hi, v_lo = halves(values)
+            stat = jnp.where(head_lane == m, jnp.where(upper, total, top), stat)
+        msg[chip, rows:] = stat
+        for copy in msg_copies(chip, 1):
+            copy.start()
+        return halves(jnp.concatenate(expos, axis=0))
+
+    def attend_values(t, u, expos):
+        chip = chip_at(t, u)
+        await_other(chip, 1)
+        e_hi, e_lo = expos
+        v_hi, v_lo = halves(v_buf[pl.ds(2 * chip, 2)].reshape(wide, cols))
         out = dot_nt(e_hi, v_hi) + (dot_nt(e_hi, v_lo) + dot_nt(e_lo, v_hi))
         part = out[:rows]
         for m in range(1, chip_heads):
             part = jnp.where(head_lane == m, out[m * rows : (m + 1) * rows], part)
         msg[chip, :rows] = part
-        msg[chip, rows:] = part_stat
-        for copy in msg_copies(chip):
+        for copy in msg_copies(chip, 0):
             copy.start()
+
+    def attend(t, u):
+        attend_values(t, u, attend_keys(t, u))
 
     def combine(t, u):
         chip = chip_at(t, u)
-        for copy in msg_copies(chip):
+        for copy in msg_copies(chip, 0) + msg_copies(chip, 1):
             copy.wait()
         every = [msg[chip]] + [msg_in[k, chip] for k in range(n_col - 1)]
         stats = [e[rows:] for e in every]
@@ -318,29 +380,35 @@
 
         lax.fori_loop(0, 2, one, 0)
 
-    bias_groups(0)
+    cut = (0, groups // 2, 5 * groups // 6, groups)
+    lax.fori_loop(cut[0], cut[1], bias_group, 0)
     event(1, 0)
-    bias_groups(1)
+    lax.fori_loop(cut[1], cut[2], bias_group, 0)
     event(1, 1)
-    bias_groups(2)
+    lax.fori_loop(cut[2], cut[3], bias_group, 0)
     for k in range(1, n_col):
         source = lax.rem(col - k + n_col, n_col)
         q_copy(k - 1, source).wait_recv()
     lax.fori_loop(0, heads // tile_heads, spread_queries, 0)
     load_w_out.wait()
-    for d in range(2, n_z):
-        event(d, 0)
-        stage(d - 2)
-        event(d, 1)
-    stage(n_z - 2)
+    event(2, 0)
+    stage(0)
+    event(2, 1)
+    stage(1)
+    for d in range(3, n_z):
+        for kind in range(2):
+            event(d, kind)
+            attend(d - 1, kind)
+            combine(d - 2, kind)
     attend(n_z - 1, 0)
-    combine(n_z - 2, 0)
-    for kind in range(2):
-        cross_sends(n_z - 1, kind, start, True)
-    attend(n_z - 1, 1)
-    combine(n_z - 2, 1)
+    cross_sends(n_z - 1, 0, start, True)
+    expos = attend_keys(n_z - 1, 1)
     for copy in sum_copies:
         copy.wait()
+    cross_sends(n_z - 1, 1, start, True)
+    attend_values(n_z - 1, 1, expos)
+    for u in range(2):
+        combine(n_z - 2, u)
     for u in range(2):
         combine(n_z - 1, u)
 
@@ -429,6 +497,8 @@
             line_sends(d, kind, wait_send, False)
         for d in range(n_z):
             cross_sends(d, kind, wait_send, False)
+    for d in range(n_z):
+        around_sends(d, wait_send, False)
     for k in range(n_col - 1):
         q_copy(k, col).wait_send()
 
@@ -463,11 +533,9 @@
             pltpu.VMEM((n, feats, cols), F32),
             pltpu.VMEM((n_col, rows, here), F32),
             pltpu.VMEM((heads, rows, 6 * head_dim), BF16),
-            pltpu.VMEM((heads, rows, cols), F32),
+            pltpu.VMEM((pl.cdiv(cols, LANES), heads * rows, LANES), F32),
             pltpu.VMEM((rows // group, group, cols, channels), F32),
-            pltpu.VMEM((heads * group, channels), F32),
-            pltpu.VMEM((heads * group, group * channels), BF16),
-            pltpu.VMEM((heads * group, group * channels), BF16),
+            pltpu.VMEM((2 * heads, 2 * channels), BF16),
             pltpu.VMEM((width, here), F32),
             pltpu.VMEM((2 * proj, here), F32),
             pltpu.VMEM((rows, here), F32),
@@ -480,8 +548,9 @@
             pltpu.VMEM((rows // 2, 2 * proj), F32),
             pltpu.VMEM((blocks, rows // 2, 2 * proj), F32),
             dma((n, 2)), dma((n_z, 2, 2)), dma((n_z, 2, 2)), dma((n_z, 2, 2, 2)),
+            dma((n_z, 2)),
             dma((peers,)), dma((n_col,)), dma((rows // group,)), dma((4,)),
-            dma((peers, chips)), dma((peers, chips)), dma((peers,)), dma((peers,)),
+            dma((peers, chips, 2)), dma((peers, chips, 2)), dma((peers,)), dma((peers,)),
             dma((peers,)), dma((peers,)),
             dma((n // 2 - 1,)), dma((blocks,)), dma((blocks // 2,)),
         ],

time: 72.8 us -> 69.2 us (0.951)
  Pallas kernels: 71.9 us -> 68.3 us
    pallas_call x1, Pallas kernels: 44.6 us -> 41 us  [sequence_update(): pl.pallas_call(functools.partial(sequence_kernel, n, n_col, head_dim, hea...]
where the time goes in v2:
time: 69.2 us; the launch traced here: 69 us
  Pallas kernels  68.3 us (99%)
    pallas_call x1, Pallas kernels, sequence_update(): pl.pallas_call(functools.partial(sequence_kernel, n, n_col, head_dim, hea...  41 us
    pallas_call x1, Pallas kernels, transition(): pl.pallas_call(transition_kernel, out_shape=(jax.ShapeDtypeStruct(seq_new...  27.3 us

profile of v2, /device:TPU:0, one launch (start us, length us, event | category | flops | bytes accessed | tf_op | source)
XLA Modules:
  0.0 69.0 jit_solution(7027394252260428165)
XLA Ops:
  0.6 41.0 %sequence_update.1 = (f32[48,512]{1,0:T(8,128)}, f32[48,64]{1,0:T(8,128)}, f32[384,64]{1,0:T(8,128)}) custom-call(f32[64,384]{1,0:T(8,128)} %bitcast.8, f32[64,384]{1,0:T(8,128)} %bitcast.9, f32[48,512]{1,0:T(8,128)} %q_ref.1, f32[48,384,128]{2,1,0:T(8,128)} %pair_ref.3, f32[32,128]{1,0:T(8,128)} %bitcast.10, f32[48,512]{1,0:T(8,128)} %seq_ref.1, ...), custom_call_target="tpu_custom_call" | custom-call | tf_op jit(solution)/shard_map/sequence_update/pallas_call | solution.py:522
  41.7 27.3 %transition.1 = (f32[48,512]{1,0:T(8,128)}, f32[48,384,128]{2,1,0:T(8,128)}) custom-call(f32[48,384,128]{2,1,0:T(8,128)} %pair_ref.3, f32[48,64]{1,0:T(8,128)} %get-tuple-element.5.left_ref, f32[384,64]{1,0:T(8,128)} %get-tuple-element.6.right_ref, f32[128,128]{1,0:T(8,128)} %w_outer_ref.1, f32[1,128]{1,0:T(1,128)} %bitcast.11, f32[128,512]{1,0:T(8,128)} %w_up_ref.1, ...), custom_call_target="tpu_custom_call" | custom-call | tf_op jit(solution)/shard_map/transition/pallas_call | solution.py:636
